TPU v7x, 32 devices: a whole 2x2x4 slice. The times are simulated.
32 devices in a mesh: dp: 8 (over z, x), tok: 4 (over y, core).
Axes of the slice: x: 2, y: 2, z: 4, core: 2. Of those that a mesh axis runs over, the one named last changes fastest.
Arguments:
- inputs: bfloat16 [128, 200, 384], P(('dp', 'tok')), may hold values from -6 to 6
- cotangent: bfloat16 [128, 200, 384], P(('dp', 'tok')), may hold values from -6 to 6
- lengths: int32 [128], P('dp'), may hold values from 1 to 198, 12672 in all
- w_qkv: float32 [2, 384, 1152], P(None, None, 'dp'), may hold values from -0.3125 to 0.3125
- w_proj: float32 [2, 384, 384], P(None, None, 'dp'), may hold values from -0.875 to 0.875
- w_fc1: float32 [2, 384, 1536], P(None, None, 'dp'), may hold values from -0.3125 to 0.3125
- w_fc2: float32 [2, 1536, 384], P(None, 'dp'), may hold values from -0.15625 to 0.15625
- norm_gains: float32 [2, 2, 384], P(None, None, 'dp'), may hold values from 0.5 to 1.5
- biases: float32 [2, 3840], P(None, 'dp'), may hold values from -1.75 to 1.75
- mom_qkv: float32 [2, 2, 384, 1152], P(None, None, None, 'dp'), as said below
- mom_proj: float32 [2, 2, 384, 384], P(None, None, None, 'dp'), as said below
- mom_fc1: float32 [2, 2, 384, 1536], P(None, None, None, 'dp'), as said below
- mom_fc2: float32 [2, 2, 1536, 384], P(None, None, 'dp'), as said below
- mom_gains: float32 [2, 2, 2, 384], P(None, None, None, 'dp'), as said below
- mom_biases: float32 [2, 2, 3840], P(None, None, 'dp'), as said below
Outputs:
- layer_out: bfloat16 [128, 200, 384], P(('dp', 'tok'))
- input_grad: float32 [128, 200, 384], P(('dp', 'tok'))
- grad_norm: float32 [], replicated
- state_qkv: float32 [2, 2, 384, 1152], P(None, None, None, 'dp')
- state_proj: float32 [2, 2, 384, 384], P(None, None, None, 'dp')
- state_fc1: float32 [2, 2, 384, 1536], P(None, None, None, 'dp')
- state_fc2: float32 [2, 2, 1536, 384], P(None, None, 'dp')
- state_gains: float32 [2, 2, 2, 384], P(None, None, None, 'dp')
- state_biases: float32 [2, 2, 3840], P(None, None, 'dp')
- second_moments: float32 [3548160], P('dp')
Inputs may be any that keep to these rules, and one draw needn't show every extreme that they name: Sequence i keeps its first lengths[i] slots; some sequence keeps all 198. `mom_qkv`: index 0 holds the first moment, index 1 the second moment, which is positive. `mom_proj`: index 0 holds the first moment, index 1 the second moment, which is positive. `mom_fc1`: index 0 holds the first moment, index 1 the second moment, which is positive. `mom_fc2`: index 0 holds the first moment, index 1 the second moment, which is positive. `mom_gains`: index 0 holds the first moment, index 1 the second moment, which is positive. `mom_biases`: index 0 holds the first moment, index 1 the second moment, which is positive.
All inputs are finite; a program needn't handle non-finite values. No bound on the sum of `lengths` on one device may be relied on, other than what follows from the above.
Results may differ from a plain program's by a relative error of at most 0.018.
The roundings to bfloat16 on the way count: a program that leaves them out, or rounds other values in their place, can miss the bound.
Values may be sent and summed in bfloat16 or wider, within the bound.
No kernel may reach another device: no remote copies, remote signals or barrier semaphores. Data moves between devices by JAX's collectives and lax.ppermute only.
A program may use at most 128 MiB of HBM per device.

v0:
```python
import math
import jax
import jax.numpy as jnp
from jax import lax
from jax.sharding import PartitionSpec as P

D = 384
HEADS = 6
HD = 64
FF = 1536
LAYERS = 2
STEP = 10
HALF_ROOT = 0.7071067811865476
INV_ROOT_TAU = 0.3989422804014327


def normalize(hidden):
    row_mean = jnp.mean(hidden, -1, keepdims=True)
    centered = hidden - row_mean
    variance = jnp.mean(centered * centered, -1, keepdims=True)
    inverse = lax.rsqrt(variance + 1e-06)
    return (centered * inverse, inverse)


def norm_back(grad_n, normed, inverse):
    first_mean = jnp.mean(grad_n, -1, keepdims=True)
    second_mean = jnp.mean(grad_n * normed, -1, keepdims=True)
    return inverse * (grad_n - first_mean - normed * second_mean)


def gelu_slope(pre_act):
    return (
        0.5 * (1.0 + lax.erf(pre_act * HALF_ROOT))
        + pre_act * jnp.exp(-0.5 * pre_act * pre_act) * INV_ROOT_TAU
    )


def spread_heads(tensor, axis):
    first = lax.slice_in_dim(tensor, 0, 5, axis=axis)
    last = lax.slice_in_dim(tensor, 5, 6, axis=axis)
    empty = jnp.zeros_like(last)
    return jnp.concatenate([first, empty, last, empty], axis)


def pick_heads(tensor, axis):
    first = lax.slice_in_dim(tensor, 0, 5, axis=axis)
    last = lax.slice_in_dim(tensor, 6, 7, axis=axis)
    return jnp.concatenate([first, last], axis)


def qkv_to_heads(packed):
    seq_count, slot_total = (packed.shape[0], packed.shape[1])
    sending = spread_heads(packed, 3).reshape(seq_count, slot_total, 3, 4, 2 * HD)
    arrived = lax.all_to_all(sending, "tok", split_axis=3, concat_axis=0, tiled=True)
    return arrived.reshape(4 * seq_count, slot_total, 3, 2, HD)


def out_to_rows(attended):
    batch_size, slot_total = (attended.shape[0], attended.shape[1])
    sending = attended.reshape(batch_size, slot_total, 1, 2 * HD)
    arrived = lax.all_to_all(sending, "tok", split_axis=0, concat_axis=2, tiled=True)
    return pick_heads(arrived.reshape(batch_size // 4, slot_total, 8, HD), 2)


def dout_to_heads(grad_rows):
    seq_count, slot_total = (grad_rows.shape[0], grad_rows.shape[1])
    sending = spread_heads(grad_rows, 2).reshape(seq_count, slot_total, 4, 2 * HD)
    arrived = lax.all_to_all(sending, "tok", split_axis=2, concat_axis=0, tiled=True)
    return arrived.reshape(4 * seq_count, slot_total, 2, HD)


def grads_to_rows(stacked):
    batch_size, slot_total = (stacked.shape[0], stacked.shape[1])
    sending = stacked.reshape(batch_size, slot_total, 3, 1, 2 * HD)
    arrived = lax.all_to_all(sending, "tok", split_axis=0, concat_axis=3, tiled=True)
    return pick_heads(arrived.reshape(batch_size // 4, slot_total, 3, 8, HD), 3)


def score_block(query_b, key_b, lens_block):
    scores = (
        jnp.einsum("bqhd,bkhd->bhqk", query_b, key_b, preferred_element_type=jnp.float32) * 0.125
    )
    key_mask = jnp.arange(key_b.shape[1])[None, :] < lens_block[:, None]
    return jnp.where(key_mask[:, None, None, :], scores, -1e30)


def forward_block(packed):
    stacked, lens_block = packed
    query_b = stacked[:, :, 0]
    key_b = stacked[:, :, 1]
    value_b = stacked[:, :, 2]
    scores = score_block(query_b, key_b, lens_block)
    row_max = jnp.max(scores, -1, keepdims=True)
    exp_part = jnp.exp(scores - row_max)
    summed = jnp.sum(exp_part, -1, keepdims=True)
    prob_low = (exp_part / summed).astype(jnp.bfloat16)
    result = jnp.einsum("bhqk,bkhd->bqhd", prob_low, value_b, preferred_element_type=jnp.float32)
    return (result.astype(jnp.bfloat16), (row_max + jnp.log(summed))[..., 0])


def backward_block(packed):
    stacked, lse_block, dout_block, lens_block = packed
    query_b = stacked[:, :, 0]
    key_b = stacked[:, :, 1]
    value_b = stacked[:, :, 2]
    scores = score_block(query_b, key_b, lens_block)
    prob_full = jnp.exp(scores - lse_block[..., None])
    grad_v = jnp.einsum(
        "bhqk,bqhd->bkhd",
        prob_full.astype(jnp.bfloat16),
        dout_block,
        preferred_element_type=jnp.float32,
    )
    grad_p = jnp.einsum("bqhd,bkhd->bhqk", dout_block, value_b, preferred_element_type=jnp.float32)
    inner_sum = jnp.sum(prob_full * grad_p, -1, keepdims=True)
    grad_s = (prob_full * (grad_p - inner_sum)).astype(jnp.bfloat16)
    grad_q = (
        jnp.einsum("bhqk,bkhd->bqhd", grad_s, key_b, preferred_element_type=jnp.float32) * 0.125
    )
    grad_k = (
        jnp.einsum("bhqk,bqhd->bkhd", grad_s, query_b, preferred_element_type=jnp.float32) * 0.125
    )
    return jnp.stack([grad_q, grad_k, grad_v], 2).astype(jnp.bfloat16)


def run_blocks(block_fn, arrays):
    batch_size = arrays[0].shape[0]
    folded = tuple((entry.reshape((batch_size // 4, 4) + entry.shape[1:]) for entry in arrays))
    result = lax.map(block_fn, folded)

    def unfold(folded_part):
        return folded_part.reshape((batch_size,) + folded_part.shape[2:])

    return jax.tree.map(unfold, result)


def sum_squares(tensors):
    return sum((jnp.sum(entry * entry) for entry in tensors))


def adamw(weight, moments, clipped, rate, decay):
    first_mom = 0.9 * moments[0] + 0.1 * clipped
    second_mom = 0.999 * moments[1] + 0.001 * clipped * clipped
    fixed_first = first_mom / (1.0 - 0.9**STEP)
    fixed_second = second_mom / (1.0 - 0.999**STEP)
    new_weight = weight - rate * (fixed_first / (jnp.sqrt(fixed_second) + 1e-08) + decay * weight)
    return (jnp.stack([new_weight, first_mom]), second_mom)


def on_device(
    inputs,
    cotangent,
    lengths,
    w_qkv,
    w_proj,
    w_fc1,
    w_fc2,
    norm_gains,
    biases,
    mom_qkv,
    mom_proj,
    mom_fc1,
    mom_fc2,
    mom_gains,
    mom_biases,
):
    full_qkv, full_proj, full_fc1, full_fc2, full_gains, full_biases = (
        lax.all_gather(w_qkv.astype(jnp.bfloat16), "dp", axis=2, tiled=True),
        lax.all_gather(w_proj.astype(jnp.bfloat16), "dp", axis=2, tiled=True),
        lax.all_gather(w_fc1.astype(jnp.bfloat16), "dp", axis=2, tiled=True),
        lax.all_gather(w_fc2.astype(jnp.bfloat16), "dp", axis=1, tiled=True),
        lax.all_gather(norm_gains.astype(jnp.bfloat16), "dp", axis=2, tiled=True),
        lax.all_gather(biases.astype(jnp.bfloat16), "dp", axis=1, tiled=True),
    )
    seq_count = inputs.shape[0]
    slot_total = inputs.shape[1]
    row_count = seq_count * slot_total
    tok_index = lax.axis_index("tok")
    own_lengths = lax.dynamic_slice_in_dim(lengths, tok_index * seq_count, seq_count, 0)
    positions = jnp.arange(slot_total)
    valid = (positions[None, :] < own_lengths[:, None]).reshape(row_count, 1)
    hidden = inputs.astype(jnp.float32).reshape(row_count, D)
    saved = []
    for layer_id in range(LAYERS):
        q_weight = full_qkv[layer_id]
        o_weight = full_proj[layer_id]
        up_weight = full_fc1[layer_id]
        down_weight = full_fc2[layer_id]
        gain_rows = full_gains[layer_id].astype(jnp.float32)
        bias_row = full_biases[layer_id].astype(jnp.float32)
        norm_first, inv_first = normalize(hidden)
        a_first = (norm_first * gain_rows[0] + bias_row[0:D]).astype(jnp.bfloat16)
        qkv_bias = jnp.concatenate(
            [bias_row[D : 2 * D], jnp.zeros((D,), jnp.float32), bias_row[2 * D : 3 * D]]
        )
        qkv = jnp.dot(a_first, q_weight, preferred_element_type=jnp.float32) + qkv_bias
        qkv = qkv.astype(jnp.bfloat16).reshape(seq_count, slot_total, 3, HEADS, HD)
        head_qkv = qkv_to_heads(qkv)
        attended, lse_all = run_blocks(forward_block, (head_qkv, lengths))
        att_rows = out_to_rows(attended).reshape(row_count, D)
        mid_hidden = (
            hidden
            + jnp.dot(att_rows, o_weight, preferred_element_type=jnp.float32)
            + bias_row[3 * D : 4 * D]
        )
        norm_second, inv_second = normalize(mid_hidden)
        a_second = (norm_second * gain_rows[1] + bias_row[4 * D : 5 * D]).astype(jnp.bfloat16)
        pre_act = (
            jnp.dot(a_second, up_weight, preferred_element_type=jnp.float32) + bias_row[6 * D :]
        )
        activated = jax.nn.gelu(pre_act, approximate=False).astype(jnp.bfloat16)
        hidden = (
            mid_hidden
            + jnp.dot(activated, down_weight, preferred_element_type=jnp.float32)
            + bias_row[5 * D : 6 * D]
        )
        saved.append(
            (
                norm_first,
                inv_first,
                a_first,
                head_qkv,
                lse_all,
                att_rows,
                norm_second,
                inv_second,
                a_second,
                pre_act,
                activated,
            )
        )
    layer_out = jnp.where(valid, hidden, 0.0).astype(jnp.bfloat16).reshape(inputs.shape)
    grad_h = cotangent.astype(jnp.float32).reshape(row_count, D) * valid.astype(jnp.float32)
    list_qkv = [None] * LAYERS
    list_proj = [None] * LAYERS
    list_fc1 = [None] * LAYERS
    list_fc2 = [None] * LAYERS
    list_gains = [None] * LAYERS
    list_biases = [None] * LAYERS
    for layer_id in range(LAYERS - 1, -1, -1):
        (
            norm_first,
            inv_first,
            a_first,
            head_qkv,
            lse_all,
            att_rows,
            norm_second,
            inv_second,
            a_second,
            pre_act,
            activated,
        ) = saved[layer_id]
        q_weight = full_qkv[layer_id]
        o_weight = full_proj[layer_id]
        up_weight = full_fc1[layer_id]
        down_weight = full_fc2[layer_id]
        gain_rows = full_gains[layer_id].astype(jnp.float32)
        grad_m = grad_h.astype(jnp.bfloat16)
        list_fc2[layer_id] = jnp.einsum(
            "rf,rd->fd", activated, grad_m, preferred_element_type=jnp.float32
        )
        bias_fc2 = jnp.sum(grad_m, 0, dtype=jnp.float32)
        grad_act = jnp.einsum("rd,fd->rf", grad_m, down_weight, preferred_element_type=jnp.float32)
        grad_up = (grad_act * gelu_slope(pre_act)).astype(jnp.bfloat16)
        list_fc1[layer_id] = jnp.einsum(
            "rd,rf->df", a_second, grad_up, preferred_element_type=jnp.float32
        )
        bias_fc1 = jnp.sum(grad_up, 0, dtype=jnp.float32)
        grad_a2 = jnp.einsum("rf,df->rd", grad_up, up_weight, preferred_element_type=jnp.float32)
        gain_second = jnp.sum(grad_a2 * norm_second, 0)
        bias_ln2 = jnp.sum(grad_a2, 0)
        grad_mid = grad_h + norm_back(grad_a2 * gain_rows[1], norm_second, inv_second)
        grad_p = grad_mid.astype(jnp.bfloat16)
        list_proj[layer_id] = jnp.einsum(
            "rd,re->de", att_rows, grad_p, preferred_element_type=jnp.float32
        )
        bias_proj = jnp.sum(grad_p, 0, dtype=jnp.float32)
        grad_att = jnp.einsum("re,de->rd", grad_p, o_weight, preferred_element_type=jnp.float32)
        grad_att = grad_att.astype(jnp.bfloat16).reshape(seq_count, slot_total, HEADS, HD)
        head_dout = dout_to_heads(grad_att)
        head_grads = run_blocks(backward_block, (head_qkv, lse_all, head_dout, lengths))
        grad_qkv = grads_to_rows(head_grads).reshape(row_count, 3 * D)
        list_qkv[layer_id] = jnp.einsum(
            "rd,rc->dc", a_first, grad_qkv, preferred_element_type=jnp.float32
        )
        bias_q = jnp.sum(grad_qkv[:, 0:D], 0, dtype=jnp.float32)
        bias_v = jnp.sum(grad_qkv[:, 2 * D : 3 * D], 0, dtype=jnp.float32)
        grad_a1 = jnp.einsum("rc,dc->rd", grad_qkv, q_weight, preferred_element_type=jnp.float32)
        gain_first = jnp.sum(grad_a1 * norm_first, 0)
        bias_ln1 = jnp.sum(grad_a1, 0)
        grad_h = grad_mid + norm_back(grad_a1 * gain_rows[0], norm_first, inv_first)
        list_gains[layer_id] = jnp.stack([gain_first, gain_second])
        list_biases[layer_id] = jnp.concatenate(
            [bias_ln1, bias_q, bias_v, bias_proj, bias_ln2, bias_fc2, bias_fc1]
        )
    input_grad = grad_h.reshape(inputs.shape)
    grad_qkv_all = jnp.stack(list_qkv)
    grad_proj_all = jnp.stack(list_proj)
    grad_fc1_all = jnp.stack(list_fc1)
    grad_fc2_all = jnp.stack(list_fc2)
    grad_gain_all = jnp.stack(list_gains)
    grad_bias_all = jnp.stack(list_biases)
    masters = (w_qkv, w_proj, w_fc1, w_fc2, norm_gains, biases)
    shard_dims = (2, 2, 2, 1, 2, 1)
    dp_index = lax.axis_index("dp")
    summed = lax.psum(
        (grad_qkv_all, grad_proj_all, grad_fc1_all, grad_fc2_all, grad_gain_all, grad_bias_all),
        ("dp", "tok"),
    )
    squares = sum_squares(summed)
    shares = tuple(
        (
            lax.dynamic_slice_in_dim(
                summed_part, dp_index * owner.shape[shard_dim], owner.shape[shard_dim], shard_dim
            )
            for summed_part, owner, shard_dim in zip(summed, masters, shard_dims)
        )
    )
    grad_norm = jnp.sqrt(squares)
    limit = 0.25 * math.sqrt(LAYERS * (4 * D * D + 2 * D * FF + 8 * D + FF))
    factor = jnp.minimum(1.0, limit / (grad_norm + 1e-06))
    state_qkv, second_qkv = adamw(w_qkv, mom_qkv, shares[0] * factor, 0.08, 0.05)
    state_proj, second_proj = adamw(w_proj, mom_proj, shares[1] * factor, 0.08, 0.05)
    state_fc1, second_fc1 = adamw(w_fc1, mom_fc1, shares[2] * factor, 0.08, 0.05)
    state_fc2, second_fc2 = adamw(w_fc2, mom_fc2, shares[3] * factor, 0.08, 0.05)
    state_gains, second_gains = adamw(norm_gains, mom_gains, shares[4] * factor, 0.4, 0.0)
    state_biases, second_biases = adamw(biases, mom_biases, shares[5] * factor, 0.4, 0.0)
    second_moments = jnp.concatenate(
        [
            second_qkv.reshape(-1),
            second_proj.reshape(-1),
            second_fc1.reshape(-1),
            second_fc2.reshape(-1),
            second_gains.reshape(-1),
            second_biases.reshape(-1),
        ]
    )
    return (
        layer_out,
        input_grad,
        grad_norm,
        state_qkv,
        state_proj,
        state_fc1,
        state_fc2,
        state_gains,
        state_biases,
        second_moments,
    )


def solution(mesh):
    placed = (
        P(("dp", "tok"), None, None),
        P(("dp", "tok"), None, None),
        P("dp"),
        P(None, None, "dp"),
        P(None, None, "dp"),
        P(None, None, "dp"),
        P(None, "dp", None),
        P(None, None, "dp"),
        P(None, "dp"),
        P(None, None, None, "dp"),
        P(None, None, None, "dp"),
        P(None, None, None, "dp"),
        P(None, None, "dp", None),
        P(None, None, None, "dp"),
        P(None, None, "dp"),
    )
    return jax.shard_map(
        on_device,
        mesh=mesh,
        in_specs=placed,
        out_specs=(
            P(("dp", "tok"), None, None),
            P(("dp", "tok"), None, None),
            P(),
            P(None, None, None, "dp"),
            P(None, None, None, "dp"),
            P(None, None, None, "dp"),
            P(None, None, "dp", None),
            P(None, None, None, "dp"),
            P(None, None, "dp"),
            P("dp"),
        ),
        check_vma=False,
    )
```

profile of v0, /device:TPU:0, one launch (start us, length us, event | category | flops | bytes accessed | tf_op | source)
XLA Modules:
  0.0 898.1 jit_solution(4694405918327446632)
XLA Ops:
  9.7 27.9 %all-gather = bf16[8,480,2]{1,2,0:T(2,128)(2,1)S(1)} all-gather(bf16[1,480,2]{1,2,0:T(2,128)(2,1)S(1)} %convert_bitcast_fusion), channel_id=1, replica_groups=mesh['dp'=8,'tok'=4] {'dp'}, dimensions={0}, use_global_device_ids=true | all-gather | bytes 17280 | tf_op jit(solution)/shard_map/all_gather | solution.py:173
  38.5 31.1 %all_gather.18 = bf16[2,2,384]{1,0,2:T(2,128)(2,1)S(1)} all-gather(bf16[2,2,48]{1,0,2:T(2,128)(2,1)S(1)} %copy.330), channel_id=1, replica_groups=mesh['dp'=8,'tok'=4] {'dp'}, dimensions={2}, use_global_device_ids=true | all-gather | bytes 3456 | tf_op jit(solution)/shard_map/all_gather | solution.py:172
  73.5 4.9 slice_reduce_fusion
  83.9 5.7 reshape.586
  93.6 3.6 copy.334
  97.2 4.6 all-to-all-start
  103.4 28.1 %all-to-all-done = bf16[4,200,3,4,128]{4,1,2,0,3:T(8,128)(2,1)} async-done(((bf16[4,200,3,4,128]{4,1,2,0,3:T(8,128)(2,1)}), bf16[4,200,3,4,128]{4,1,2,0,3:T(8,128)(2,1)}, u32[]{:S(2)}, u32[]{:S(2)}) %all-to-all-start) | async-done | bytes 2457632 | tf_op jit(solution)/shard_map/all_to_all | solution.py:54
  136.3 13.3 %while.44 = (s32[]{:T(128)}, bf16[4,4,200,2,64]{2,4,3,1,0:T(8,128)(2,1)}, f32[4,4,2,200]{3,2,1,0:T(2,128)}, bf16[4,4,200,3,2,64]{2,5,4,1,3,0:T(8,128)(2,1)S(1)}, s32[4,4]{1,0:T(4,128)}, /*index=5*/s32[]{:T(128)}) while((s32[]{:T(128)}, bf16[4,4,200,2,64]{2,4,3,1,0:T(8,128)(2,1)}, f32[4,4,2,200]{3,2,1,0:T(2,128)}, ...), condition=%wide.region_5.6_spmd, body=%wide.region_2.5_spmd.sunk | while | flops 84581600 | bytes 6535325 | solution.py:129
  152.5 4.2 all-to-all-start.1
  160.9 33.1 %all_gather.21 = bf16[2,384,384]{1,2,0:T(8,128)(2,1)S(1)} all-gather(bf16[2,384,48]{1,2,0:T(8,128)(2,1)S(1)} %convert_element_type.200), channel_id=1, replica_groups=mesh['dp'=8,'tok'=4] {'dp'}, dimensions={2}, use_global_device_ids=true | all-gather | bytes 663552 | tf_op jit(solution)/shard_map/all_gather | solution.py:169
  198.3 14.6 %fusion.38 = (bf16[800,1536]{1,0:T(8,128)(2,1)}, f32[800,1536]{1,0:T(8,128)}) fusion(f32[1536]{0:T(1024)S(1)} %get-tuple-element.494, bf16[2,384,1536]{1,2,0:T(8,128)(2,1)} %all-gather.7.cloned.1.call-done, f32[800,384]{1,0:T(8,128)S(1)} %get-tuple-element.476, f32[384]{0:T(512)S(1)} %copy-done.70, f32[384]{0:T(512)S(1)} %copy-done.66, ...), kind=kOutput, calls=%fused_computation.94 | convolution fusion | flops 1026355200 | bytes 9796864 | tf_op jit(solution)/shard_map/dot_general | solution.py:209
  214.7 3.7 fusion.121
  223.2 5.7 reshape.591
  232.8 13.8 %copy.342 = bf16[4,200,3,4,128]{4,1,2,0,3:T(8,128)(2,1)} copy(bf16[4,200,3,4,128]{1,0,4,3,2:T(4,128)(2,1)S(1)} %bitcast.482) | data formatting | bytes 4915200 | tf_op jit(solution)/shard_map/reshape | solution.py:53
  246.6 4.6 all-to-all-start.2
  251.2 29.6 %all-to-all-done.2 = bf16[4,200,3,4,128]{4,1,2,0,3:T(8,128)(2,1)} async-done(((bf16[4,200,3,4,128]{4,1,2,0,3:T(8,128)(2,1)}), bf16[4,200,3,4,128]{4,1,2,0,3:T(8,128)(2,1)}, u32[]{:S(2)}, u32[]{:S(2)}) %all-to-all-start.2) | async-done | bytes 2457632 | tf_op jit(solution)/shard_map/all_to_all | solution.py:54
  285.0 8.3 while.45
  295.5 4.2 all-to-all-start.3
  302.7 9.1 %all-to-all-done.3 = bf16[16,200,1,128]{3,1,2,0:T(8,128)(2,1)} async-done(((bf16[16,200,1,128]{3,1,2,0:T(8,128)(2,1)}), bf16[16,200,1,128]{3,1,2,0:T(8,128)(2,1)}, u32[]{:S(2)}, u32[]{:S(2)}) %all-to-all-start.3) | async-done | bytes 819232 | tf_op jit(solution)/shard_map/all_to_all | solution.py:61
  323.4 12.8 %fusion.41 = (bf16[800,1536]{1,0:T(8,128)(2,1)}, f32[800,1536]{1,0:T(8,128)S(1)}) fusion(f32[1536]{0:T(1024)S(1)} %copy-done.85, bf16[2,384,1536]{1,2,0:T(8,128)(2,1)S(1)} %copy-done.111, f32[800,384]{1,0:T(8,128)S(1)} %get-tuple-element.482, f32[384]{0:T(512)S(1)} %copy-done.72, f32[384]{0:T(512)S(1)} %copy-done.65, f32[800]{0:T(1024)S(1)} %add_rsqrt_fusion, ...), kind=kOutput, calls=%fused_computation.97 | convolution fusion | flops 1026355200 | bytes 9801728 | tf_op jit(solution)/shard_map/dot_general | solution.py:209
  336.1 4.3 convert_reduce_fusion
  358.5 4.2 all-to-all-start.4
  362.7 12.1 %all-to-all-done.4 = bf16[4,200,4,128]{3,1,0,2:T(8,128)(2,1)} async-done(((bf16[4,200,4,128]{3,1,0,2:T(8,128)(2,1)}), bf16[4,200,4,128]{3,1,0,2:T(8,128)(2,1)}, u32[]{:S(2)}, u32[]{:S(2)}) %all-to-all-start.4) | async-done | bytes 819232 | tf_op jit(solution)/shard_map/all_to_all | solution.py:68
  379.1 23.6 %while.46 = (s32[]{:T(128)}, bf16[4,4,200,3,2,64]{2,5,4,3,1,0:T(8,128)(2,1)}, bf16[4,4,200,3,2,64]{2,5,4,1,3,0:T(8,128)(2,1)S(1)}, s32[4,4]{1,0:T(4,128)S(1)}, f...) while((s32[]{:T(128)}, bf16[4,4,200,3,2,64]{2,5,4,3,1,0:T(8,128)(2,1)}, ...), condition=%wide.region_20.21_spmd, body=%wide.region_18.20_spmd.sunk | while | flops 208805600 | bytes 15433129 | solution.py:129
  402.7 4.6 copy.354
  407.2 4.7 all-to-all-start.5
  411.9 4.7 convolution_bitcast_fusion.2
  416.6 24.9 %all-to-all-done.5 = bf16[16,200,3,1,128]{4,1,3,2,0:T(8,128)(2,1)} async-done(((bf16[16,200,3,1,128]{4,1,3,2,0:T(8,128)(2,1)}), bf16[16,200,3,1,128]{4,1,3,2,0:T(8,128)(2,1)}, u32[]{:S(2)}, u32[]{:S(2)}) %all-to-all-start.5) | async-done | bytes 2457632 | tf_op jit(solution)/shard_map/all_to_all | solution.py:75
  441.6 4.6 copy.355
  452.7 5.5 reshape.600
  458.2 4.1 multiply_reduce_fusion.6
  464.0 5.9 convert_reduce_fusion.1
  482.5 4.2 all-to-all-start.6
  486.7 5.1 convolution_bitcast_fusion
  494.9 3.9 all-to-all-done.6
  502.2 23.0 %while.47 = (s32[]{:T(128)}, bf16[4,4,200,3,2,64]{2,5,4,3,1,0:T(8,128)(2,1)}, bf16[4,4,200,3,2,64]{2,5,4,1,3,0:T(8,128)(2,1)}, s32[4,4]{1,0:T(4,128)S(1)}, f32[4...) while((s32[]{:T(128)}, bf16[4,4,200,3,2,64]{2,5,4,3,1,0:T(8,128)(2,1)}, ...), condition=%wide.region_27.28_spmd, body=%wide.region_25.27_spmd.sunk | while | flops 208805600 | bytes 15790513 | solution.py:129
  525.3 4.6 copy.363
  529.9 4.6 all-to-all-start.7
  534.6 5.0 convolution_bitcast_fusion.4
  548.2 16.0 %all-to-all-done.7 = bf16[16,200,3,1,128]{4,1,3,2,0:T(8,128)(2,1)} async-done(((bf16[16,200,3,1,128]{4,1,3,2,0:T(8,128)(2,1)}), bf16[16,200,3,1,128]{4,1,3,2,0:T(8,128)(2,1)}, u32[]{:S(2)}, u32[]{:S(2)}) %all-to-all-start.7) | async-done | bytes 2457632 | tf_op jit(solution)/shard_map/all_to_all | solution.py:75
  564.1 4.7 copy.364
  575.3 4.5 reshape.604
  600.1 4.5 fusion.77
  607.9 41.2 %all-reduce = (f32[2,2,384]{2,1,0:T(2,128)S(1)}, f32[2,3840]{1,0:T(2,128)S(1)}) all-reduce(f32[2,2,384]{2,1,0:T(2,128)S(1)} %pad_maximum_fusion.26, f32[2,3840]{1,0:T(2,128)S(1)} %pad_maximum_fusion.22), channel_id=1, replica_groups=mesh['dp'=8,'tok'=4] {'dp','tok'}, use_global_device_ids=true, to_apply=%region_42.43 | all-reduce | flops 9216 | bytes 73728 | tf_op jit(solution)/shard_map/psum | solution.py:307
  653.2 179.8 %all-reduce.4.cloned.1.call-done = (f32[2,384,1152]{2,1,0:T(8,128)}, f32[2,384,384]{2,1,0:T(8,128)}, f32[2,384,1536]{2,1,0:T(8,128)}, f32[2,1536,384]{2,1,0:T(8,128)}) async-done(((f32[2,384,1152]{2,1,0:T(8,128)}, f32[2,384,384]{2,1,0:T(8,128)}, f32[2,384,1536]{2,1,0:T(8,128)}, f32[2,1536,384]{2,1,0:T(8,128)}), (f32[2,384,1152]{2,1,0:T(8,128)}, f32[2,384,384]{2,1,0:T(8,128)}, f32[2,384,1536]{2,1,0:T(8,128)}, ...) | async-done | bytes 14155792 | tf_op jit(solution)/shard_map/psum | solution.py:307
  835.3 3.5 multiply_reduce_fusion.4
  853.7 3.6 subtract_bitcast_fusion
  877.9 12.1 %concatenate.67 = f32[443520]{0:T(1024)} concatenate(f32[110592]{0:T(1024)S(1)} %copy-done.47, f32[36864]{0:T(1024)S(1)} %copy-done.54, f32[147456]{0:T(1024)S(1)} %copy-done.42, f32[147456]{0:T(1024)S(1)} %copy-done.41, f32[192]{0:T(256)S(1)} %copy-done.92, f32[960]{0:T(1024)S(1)} %reshape.611), dimensions={0} | concatenate | bytes 3548160 | tf_op jit(solution)/shard_map/concatenate | solution.py:329
  (578 shorter events, 258.9 us)
Async XLA Ops:
  7.2 65.6 %copy-start.1 = (bf16[4,200,384]{2,1,0:T(8,128)(2,1)S(1)}, bf16[4,200,384]{2,1,0:T(8,128)(2,1)}, u32[]{:S(2)}) copy-start(bf16[4,200,384]{2,1,0:T(8,128)(2,1)} %param.23) | copy-start | bytes 1843204
  7.2 71.7 %all-gather.5.cloned.1.call-start = ((), (), s32[]{:S(2)}) async-start(), calls=%async_computation.8 | async-start | bytes 1990656 | tf_op jit(solution)/shard_map/all_gather | solution.py:168
  69.6 9.2 %copy-start.64 = (f32[1,3840]{1,0:T(1,128)}, f32[1,3840]{1,0:T(1,128)S(1)}, u32[]{:S(2)}) copy-start(f32[1,3840]{1,0:T(1,128)S(1)} %get-tuple-element.470) | copy-start | bytes 46084
  72.8 6.1 copy-start.62
  97.2 5.5 copy-start.107
  97.2 34.3 %all-to-all-start = ((bf16[4,200,3,4,128]{4,1,2,0,3:T(8,128)(2,1)}), bf16[4,200,3,4,128]{4,1,2,0,3:T(8,128)(2,1)}, u32[]{:S(2)}, u32[]{:S(2)}) async-start(bf16[4,200,3,4,128]{4,1,2,0,3:T(8,128)(2,1)} %copy.334), calls=%async_computation | async-start | bytes 4915200 | tf_op jit(solution)/shard_map/all_to_all | solution.py:54
  101.9 96.3 %all-gather.7.cloned.1.call-start = ((), (), s32[]{:S(2)}) async-start(), calls=%async_computation.9 | async-start | bytes 2654208 | tf_op jit(solution)/shard_map/all_gather | solution.py:170
  149.6 9.0 %copy-start = (bf16[4,4,200,3,2,64]{2,5,4,1,3,0:T(8,128)(2,1)}, bf16[4,4,200,3,2,64]{2,5,4,1,3,0:T(8,128)(2,1)S(1)}, u32[]{:S(2)}) copy-start(bf16[4,4,200,3,2,64]{2,5,4,1,3,0:T(8,128)(2,1)S(1)} %get-tuple-element.738) | copy-start | bytes 7372804
  152.5 41.4 %all-to-all-start.1 = ((bf16[16,200,1,128]{3,1,2,0:T(8,128)(2,1)}), bf16[16,200,1,128]{3,1,2,0:T(8,128)(2,1)}, u32[]{:S(2)}, u32[]{:S(2)}) async-start(bf16[16,200,1,128]{3,1,2,0:T(8,128)(2,1)} %copy.337), calls=%async_computation.1 | async-start | bytes 1638400 | tf_op jit(solution)/shard_map/all_to_all | solution.py:61
  156.7 58.0 %all-gather.9.cloned.1.call-start = ((), (), s32[]{:S(2)}) async-start(), calls=%async_computation.10 | async-start | bytes 2654208 | tf_op jit(solution)/shard_map/all_gather | solution.py:171
  160.9 37.4 %copy-start.83 = (f32[1536]{0:T(1024)}, f32[1536]{0:T(1024)S(1)}, u32[]{:S(2)}) copy-start(f32[1536]{0:T(1024)S(1)} %get-tuple-element.494) | copy-start | bytes 18436
  197.8 16.9 %copy-start.4 = (f32[800,384]{1,0:T(8,128)}, f32[800,384]{1,0:T(8,128)S(1)}, u32[]{:S(2)}) copy-start(f32[800,384]{1,0:T(8,128)S(1)} %get-tuple-element.476) | copy-start | bytes 3686404
  197.8 15.0 %copy-start.58 = (f32[800]{0:T(1024)}, f32[800]{0:T(1024)S(1)}, u32[]{:S(2)}) copy-start(f32[800]{0:T(1024)S(1)} %broadcast_multiply_fusion.10) | copy-start | bytes 9604
  198.2 14.7 %copy-start.60 = (f32[800]{0:T(1024)}, f32[800]{0:T(1024)S(1)}, u32[]{:S(2)}) copy-start(f32[800]{0:T(1024)S(1)} %add_rsqrt_fusion.2) | copy-start | bytes 9604
  198.3 16.4 %copy-start.106 = (f32[384]{0:T(512)S(1)}, f32[384]{0:T(512)}, u32[]{:S(2)}) copy-start(f32[384]{0:T(512)} %get-tuple-element.370) | copy-start | bytes 4612
  246.6 34.2 %all-to-all-start.2 = ((bf16[4,200,3,4,128]{4,1,2,0,3:T(8,128)(2,1)}), bf16[4,200,3,4,128]{4,1,2,0,3:T(8,128)(2,1)}, u32[]{:S(2)}, u32[]{:S(2)}) async-start(bf16[4,200,3,4,128]{4,1,2,0,3:T(8,128)(2,1)} %copy.342), calls=%async_computation.2 | async-start | bytes 4915200 | tf_op jit(solution)/shard_map/all_to_all | solution.py:54
  251.2 33.8 %copy-start.96 = (s32[4,4]{1,0:T(4,128)S(1)}, s32[4,4]{1,0:T(4,128)}, u32[]{:S(2)}) copy-start(s32[4,4]{1,0:T(4,128)} %get-tuple-element.772) | copy-start | bytes 196
  293.3 6.5 copy-start.108
  295.5 16.3 %all-to-all-start.3 = ((bf16[16,200,1,128]{3,1,2,0:T(8,128)(2,1)}), bf16[16,200,1,128]{3,1,2,0:T(8,128)(2,1)}, u32[]{:S(2)}, u32[]{:S(2)}) async-start(bf16[16,200,1,128]{3,1,2,0:T(8,128)(2,1)} %copy.345), calls=%async_computation.3 | async-start | bytes 1638400 | tf_op jit(solution)/shard_map/all_to_all | solution.py:61
  300.0 15.2 %copy-start.93 = (pred[800]{0:T(1024)(128)(4,1)}, pred[800]{0:T(1024)(128)(4,1)S(1)}, u32[]{:S(2)}) copy-start(pred[800]{0:T(1024)(128)(4,1)S(1)} %lt.134) | copy-start | bytes 2404
  323.0 19.7 %copy-start.6 = (f32[800,384]{1,0:T(8,128)}, f32[800,384]{1,0:T(8,128)S(1)}, u32[]{:S(2)}) copy-start(f32[800,384]{1,0:T(8,128)S(1)} %get-tuple-element.482) | copy-start | bytes 3686404
  323.4 12.8 %copy-start.53 = (bf16[4,200,384]{2,1,0:T(8,128)(2,1)S(1)}, bf16[4,200,384]{2,1,0:T(8,128)(2,1)}, u32[]{:S(2)}) copy-start(bf16[4,200,384]{2,1,0:T(8,128)(2,1)} %get-tuple-element.444) | copy-start | bytes 1843204
  323.4 12.8 %copy-start.109 = (bf16[2,1536,384]{2,1,0:T(8,128)(2,1)S(1)}, bf16[2,1536,384]{2,1,0:T(8,128)(2,1)}, u32[]{:S(2)}) copy-start(bf16[2,1536,384]{2,1,0:T(8,128)(2,1)} %all-gather.9.cloned.1.call-done) | copy-start | bytes 7077892
  358.5 16.3 %all-to-all-start.4 = ((bf16[4,200,4,128]{3,1,0,2:T(8,128)(2,1)}), bf16[4,200,4,128]{3,1,0,2:T(8,128)(2,1)}, u32[]{:S(2)}, u32[]{:S(2)}) async-start(bf16[4,200,4,128]{3,1,0,2:T(8,128)(2,1)} %copy.350), calls=%async_computation.4 | async-start | bytes 1638400 | tf_op jit(solution)/shard_map/all_to_all | solution.py:68
  407.2 34.3 %all-to-all-start.5 = ((bf16[16,200,3,1,128]{4,1,3,2,0:T(8,128)(2,1)}), bf16[16,200,3,1,128]{4,1,3,2,0:T(8,128)(2,1)}, u32[]{:S(2)}, u32[]{:S(2)}) async-start(bf16[16,200,3,1,128]{4,1,3,2,0:T(8,128)(2,1)} %copy.354), calls=%async_computation.5 | async-start | bytes 4915200 | tf_op jit(solution)/shard_map/all_to_all | solution.py:75
  452.7 5.5 copy-start.15
  463.5 8.6 copy-start.28
  464.0 5.9 copy-start.5
  464.0 5.9 copy-start.59
  464.0 5.9 copy-start.61
  464.0 5.9 copy-start.67
  464.0 5.9 copy-start.112
  482.5 16.3 %all-to-all-start.6 = ((bf16[4,200,4,128]{3,1,0,2:T(8,128)(2,1)}), bf16[4,200,4,128]{3,1,0,2:T(8,128)(2,1)}, u32[]{:S(2)}, u32[]{:S(2)}) async-start(bf16[4,200,4,128]{3,1,0,2:T(8,128)(2,1)} %copy.359), calls=%async_computation.6 | async-start | bytes 1638400 | tf_op jit(solution)/shard_map/all_to_all | solution.py:68
  486.7 5.1 copy-start.13
  486.7 5.1 copy-start.20
  529.9 34.3 %all-to-all-start.7 = ((bf16[16,200,3,1,128]{4,1,3,2,0:T(8,128)(2,1)}), bf16[16,200,3,1,128]{4,1,3,2,0:T(8,128)(2,1)}, u32[]{:S(2)}, u32[]{:S(2)}) async-start(bf16[16,200,3,1,128]{4,1,3,2,0:T(8,128)(2,1)} %copy.363), calls=%async_computation.7 | async-start | bytes 4915200 | tf_op jit(solution)/shard_map/all_to_all | solution.py:75
  534.5 298.5 %all-reduce.4.cloned.1.call-start = ((), (), s32[]{:S(2)}) async-start(), calls=%async_computation.11 | async-start | bytes 28311552 | tf_op jit(solution)/shard_map/psum | solution.py:307
  534.6 5.0 copy-start.29
  534.6 5.0 copy-start.115
  600.0 5.0 copy-start.24
  607.4 43.0 %copy-start.10 = (f32[800,384]{1,0:T(8,128)S(1)}, f32[800,384]{1,0:T(8,128)}, u32[]{:S(2)}) copy-start(f32[800,384]{1,0:T(8,128)} %copy-done.8) | copy-start | bytes 3686404
  833.0 5.8 copy-start.17
  841.2 5.7 copy-start.75
  841.2 5.7 copy-start.91
  841.2 5.9 copy-start.86
  841.2 5.9 copy-start.95
  848.4 5.3 copy-start.31
  848.4 5.3 copy-start.32
  (81 other events, 238.9 us)
Sparse Core Ops, SparseCore 0:
  10.9 50.0 all-gather.4
  105.5 51.8 all-gather.6
  160.3 54.3 all-gather.8
  585.1 247.8 all-reduce.3
where the time goes:
time: 911 us; the launch traced here: 898 us
  waiting for transfers between devices  305 us (33%)
  local copies, waits for them, and re-layouts  189 us (21%)
  blocking collectives  133 us (15%)
  matrix products  127 us (14%)
  other arithmetic  86.8 us (10%)
  starting transfers between devices  35.5 us (4%)
  between operations  20.9 us (2%)
    psum x1, waiting for transfers between devices, on_device(): lax.psum((grad_qkv_all, grad_proj_all, grad_fc1_all, grad_fc2_all, grad_g...  180 us
    all_to_all x2, waiting for transfers between devices, qkv_to_heads(): lax.all_to_all(sending, 'tok', split_axis=3, concat_axis=0, tiled=True)  57.7 us
    psum x1, blocking collectives, on_device(): lax.psum((grad_qkv_all, grad_proj_all, grad_fc1_all, grad_fc2_all, grad_g...  41.2 us
    all_to_all x2, waiting for transfers between devices, grads_to_rows(): lax.all_to_all(sending, 'tok', split_axis=0, concat_axis=3, tiled=True)  40.9 us
    all_gather x1, blocking collectives, on_device(): lax.all_gather(w_proj.astype(jnp.bfloat16), 'dp', axis=2, tiled=True)  33.1 us
    all_gather x1, blocking collectives, on_device(): lax.all_gather(norm_gains.astype(jnp.bfloat16), 'dp', axis=2, tiled=True)  31.1 us
    all_gather x1, blocking collectives, on_device(): lax.all_gather(biases.astype(jnp.bfloat16), 'dp', axis=1, tiled=True)  27.9 us
    dot_general x2, matrix products, on_device(): jnp.dot(a_second, up_weight, preferred_element_type=jnp.float32)  27.4 us
  transfers between devices with their start and end apart: 12, of which 9 were waited for; matrix products, arithmetic and copies ran while one was open for 12% of the time, Pallas kernels for 0%

commit v1 on v0

--- a/solution.py
+++ b/solution.py
@@ -305,8 +305,11 @@
     shard_dims = (2, 2, 2, 1, 2, 1)
     dp_index = lax.axis_index("dp")
     summed = lax.psum(
-        (grad_qkv_all, grad_proj_all, grad_fc1_all, grad_fc2_all, grad_gain_all, grad_bias_all),
-        ("dp", "tok"),
+        lax.psum(
+            (grad_qkv_all, grad_proj_all, grad_fc1_all, grad_fc2_all, grad_gain_all, grad_bias_all),
+            "tok",
+        ),
+        "dp",
     )
     squares = sum_squares(summed)
     shares = tuple(

time: 911 us -> 1360 us (1.49)
  waiting for transfers between devices: 305 us -> 736 us
    psum x0 -> x1, waiting for transfers between devices: none -> 367 us  [on_device(): lax.psum(lax.psum((grad_qkv_all, grad_proj_all, grad_fc1_all, grad_fc2_al...]
    psum x1, waiting for transfers between devices: 180 us -> 245 us  [on_device(): lax.psum((grad_qkv_all, grad_proj_all, grad_fc1_all, grad_fc2_all, grad_g...]
    psum x0 -> x1, blocking collectives: none -> 40.9 us  [on_device(): lax.psum(lax.psum((grad_qkv_all, grad_proj_all, grad_fc1_all, grad_fc2_al...]
    psum x1, blocking collectives: 41.2 us -> 11.5 us  [on_device(): lax.psum((grad_qkv_all, grad_proj_all, grad_fc1_all, grad_fc2_all, grad_g...]
  transfers between devices with their start and end apart: 12 -> 13, of which waited for: 9 -> 9; matrix products, arithmetic and copies ran while one was open for 12% -> 8% of each run, Pallas kernels for 0% -> 0%
where the time goes in v1:
time: 1360 us; the launch traced here: 1340 us
  waiting for transfers between devices  736 us (54%)
  local copies, waits for them, and re-layouts  182 us (13%)
  blocking collectives  144 us (11%)
  matrix products  127 us (9%)
  other arithmetic  96.7 us (7%)
  starting transfers between devices  36 us (3%)
  between operations  21 us (2%)
    psum x1, waiting for transfers between devices, on_device(): lax.psum(lax.psum((grad_qkv_all, grad_proj_all, grad_fc1_all, grad_fc2_al...  367 us
    psum x1, waiting for transfers between devices, on_device(): lax.psum((grad_qkv_all, grad_proj_all, grad_fc1_all, grad_fc2_all, grad_g...  245 us
    all_to_all x2, waiting for transfers between devices, qkv_to_heads(): lax.all_to_all(sending, 'tok', split_axis=3, concat_axis=0, tiled=True)  57.7 us
    psum x1, blocking collectives, on_device(): lax.psum(lax.psum((grad_qkv_all, grad_proj_all, grad_fc1_all, grad_fc2_al...  40.9 us
    all_to_all x2, waiting for transfers between devices, grads_to_rows(): lax.all_to_all(sending, 'tok', split_axis=0, concat_axis=3, tiled=True)  40.6 us
    all_gather x1, blocking collectives, on_device(): lax.all_gather(w_proj.astype(jnp.bfloat16), 'dp', axis=2, tiled=True)  33.1 us
    all_gather x1, blocking collectives, on_device(): lax.all_gather(norm_gains.astype(jnp.bfloat16), 'dp', axis=2, tiled=True)  31.1 us
    all_gather x1, blocking collectives, on_device(): lax.all_gather(biases.astype(jnp.bfloat16), 'dp', axis=1, tiled=True)  27.9 us
  transfers between devices with their start and end apart: 13, of which 9 were waited for; matrix products, arithmetic and copies ran while one was open for 8% of the time, Pallas kernels for 0%

profile of v1, /device:TPU:0, one launch (start us, length us, event | category | flops | bytes accessed | tf_op | source)
XLA Modules:
  0.0 1342.6 jit_solution(11258011042699468094)
XLA Ops:
  9.7 27.9 %all-gather = bf16[8,480,2]{1,2,0:T(2,128)(2,1)S(1)} all-gather(bf16[1,480,2]{1,2,0:T(2,128)(2,1)S(1)} %convert_bitcast_fusion), channel_id=1, replica_groups=mesh['dp'=8,'tok'=4] {'dp'}, dimensions={0}, use_global_device_ids=true | all-gather | bytes 17280 | tf_op jit(solution)/shard_map/all_gather | solution.py:173
  38.5 31.1 %all_gather.18 = bf16[2,2,384]{1,0,2:T(2,128)(2,1)S(1)} all-gather(bf16[2,2,48]{1,0,2:T(2,128)(2,1)S(1)} %copy.330), channel_id=1, replica_groups=mesh['dp'=8,'tok'=4] {'dp'}, dimensions={2}, use_global_device_ids=true | all-gather | bytes 3456 | tf_op jit(solution)/shard_map/all_gather | solution.py:172
  73.5 4.9 slice_reduce_fusion
  83.9 5.7 reshape.586
  97.2 4.6 all-to-all-start
  103.4 28.1 %all-to-all-done = bf16[4,200,3,4,128]{4,1,2,0,3:T(8,128)(2,1)} async-done(((bf16[4,200,3,4,128]{4,1,2,0,3:T(8,128)(2,1)}), bf16[4,200,3,4,128]{4,1,2,0,3:T(8,128)(2,1)}, u32[]{:S(2)}, u32[]{:S(2)}) %all-to-all-start) | async-done | bytes 2457632 | tf_op jit(solution)/shard_map/all_to_all | solution.py:54
  136.3 13.3 while.44
  152.5 4.2 all-to-all-start.1
  160.9 33.1 %all_gather.21 = bf16[2,384,384]{1,2,0:T(8,128)(2,1)S(1)} all-gather(bf16[2,384,48]{1,2,0:T(8,128)(2,1)S(1)} %convert_element_type.200), channel_id=1, replica_groups=mesh['dp'=8,'tok'=4] {'dp'}, dimensions={2}, use_global_device_ids=true | all-gather | bytes 663552 | tf_op jit(solution)/shard_map/all_gather | solution.py:169
  200.6 14.6 %fusion.38 = (bf16[800,1536]{1,0:T(8,128)(2,1)}, f32[800,1536]{1,0:T(8,128)}) fusion(f32[1536]{0:T(1024)S(1)} %get-tuple-element.500, bf16[2,384,1536]{1,2,0:T(8,128)(2,1)} %all-gather.7.cloned.1.call-done, f32[800,384]{1,0:T(8,128)S(1)} %get-tuple-element.482, f32[384]{0:T(512)S(1)} %copy-done.72, f32[384]{0:T(512)S(1)} %copy-done.68, ...), kind=kOutput, calls=%fused_computation.94 | convolution fusion | flops 1026355200 | bytes 9796864 | tf_op jit(solution)/shard_map/dot_general | solution.py:209
  215.3 3.7 fusion.121
  223.8 5.7 reshape.591
  230.5 13.7 %pad_maximum_fusion.4 = bf16[4,200,3,8,64]{1,0,4,3,2:T(4,128)(2,1)S(1)} fusion(bf16[4,200,3,1,64]{1,0,4,3,2:T(4,128)(2,1)S(1)} %broadcast.401, bf16[4,200,3,1,64]{1,0,4,3,2:T(4,128)(2,1)S(1)} %slice.397, bf16[4,200,3,5,64]{1,0,4,3,2:T(4,128)(2,1)S(1)} %slice.396), kind=kLoop, calls=%fused_computation.148 | loop fusion | flops 3686400 | bytes 4608000 | tf_op jit(solution)/shard_map/concatenate | solution.py:42
  244.2 3.7 copy.342
  247.8 4.6 all-to-all-start.2
  252.4 29.6 %all-to-all-done.2 = bf16[4,200,3,4,128]{4,1,2,0,3:T(8,128)(2,1)} async-done(((bf16[4,200,3,4,128]{4,1,2,0,3:T(8,128)(2,1)}), bf16[4,200,3,4,128]{4,1,2,0,3:T(8,128)(2,1)}, u32[]{:S(2)}, u32[]{:S(2)}) %all-to-all-start.2) | async-done | bytes 2457632 | tf_op jit(solution)/shard_map/all_to_all | solution.py:54
  286.2 8.3 while.45
  296.7 4.2 all-to-all-start.3
  303.9 9.1 all-to-all-done.3
  324.6 12.8 fusion.41
  337.3 4.3 convert_reduce_fusion
  359.1 4.2 all-to-all-start.4
  363.3 12.1 all-to-all-done.4
  379.7 23.5 %while.46 = (s32[]{:T(128)}, bf16[4,4,200,3,2,64]{2,5,4,3,1,0:T(8,128)(2,1)}, bf16[4,4,200,3,2,64]{2,5,4,1,3,0:T(8,128)(2,1)S(1)}, s32[4,4]{1,0:T(4,128)S(1)}, f...) while((s32[]{:T(128)}, bf16[4,4,200,3,2,64]{2,5,4,3,1,0:T(8,128)(2,1)}, ...), condition=%wide.region_20.21_spmd, body=%wide.region_18.20_spmd.sunk | while | flops 208805600 | bytes 15433129 | solution.py:129
  403.2 4.6 copy.354
  407.8 4.7 all-to-all-start.5
  412.5 4.7 convolution_bitcast_fusion.2
  417.2 24.9 %all-to-all-done.5 = bf16[16,200,3,1,128]{4,1,3,2,0:T(8,128)(2,1)} async-done(((bf16[16,200,3,1,128]{4,1,3,2,0:T(8,128)(2,1)}), bf16[16,200,3,1,128]{4,1,3,2,0:T(8,128)(2,1)}, u32[]{:S(2)}, u32[]{:S(2)}) %all-to-all-start.5) | async-done | bytes 2457632 | tf_op jit(solution)/shard_map/all_to_all | solution.py:75
  442.1 4.6 copy.355
  453.3 5.5 reshape.600
  458.8 4.1 multiply_reduce_fusion.6
  464.6 5.9 convert_reduce_fusion.1
  483.0 4.2 all-to-all-start.6
  487.2 5.1 convolution_bitcast_fusion
  495.4 3.9 all-to-all-done.6
  502.8 23.0 %while.47 = (s32[]{:T(128)}, bf16[4,4,200,3,2,64]{2,5,4,3,1,0:T(8,128)(2,1)}, bf16[4,4,200,3,2,64]{2,5,4,1,3,0:T(8,128)(2,1)}, s32[4,4]{1,0:T(4,128)S(1)}, f32[4...) while((s32[]{:T(128)}, bf16[4,4,200,3,2,64]{2,5,4,3,1,0:T(8,128)(2,1)}, ...), condition=%wide.region_27.28_spmd, body=%wide.region_25.27_spmd.sunk | while | flops 208805600 | bytes 15790513 | solution.py:129
  525.7 4.6 copy.363
  530.3 4.6 all-to-all-start.7
  535.3 5.0 convolution_bitcast_fusion.4
  548.8 15.7 %all-to-all-done.7 = bf16[16,200,3,1,128]{4,1,3,2,0:T(8,128)(2,1)} async-done(((bf16[16,200,3,1,128]{4,1,3,2,0:T(8,128)(2,1)}), bf16[16,200,3,1,128]{4,1,3,2,0:T(8,128)(2,1)}, u32[]{:S(2)}, u32[]{:S(2)}) %all-to-all-start.7) | async-done | bytes 2457632 | tf_op jit(solution)/shard_map/all_to_all | solution.py:75
  564.6 4.5 copy.364
  575.6 5.5 reshape.604
  586.4 245.1 %all-reduce.9.cloned.1.call-done = (f32[2,384,1152]{2,1,0:T(8,128)}, f32[2,384,384]{2,1,0:T(8,128)}, f32[2,384,1536]{2,1,0:T(8,128)}, f32[2,1536,384]{2,1,0:T(8,128)}) async-done(((f32[2,384,1152]{2,1,0:T(8,128)}, f32[2,384,384]{2,1,0:T(8,128)}, f32[2,384,1536]{2,1,0:T(8,128)}, f32[2,1536,384]{2,1,0:T(8,128)}), (f32[2,384,1152]{2,1,0:T(8,128)}, f32[2,384,384]{2,1,0:T(8,128)}, f32[2,384,1536]{2,1,0:T(8,128)}, ...) | async-done | bytes 14155792 | tf_op jit(solution)/shard_map/psum | solution.py:308
  846.3 4.4 fusion.77
  854.2 11.5 all-reduce.2
  865.7 40.9 %all-reduce = (f32[2,2,384]{2,1,0:T(2,128)S(1)}, f32[2,3840]{1,0:T(2,128)S(1)}) all-reduce(f32[2,2,384]{2,1,0:T(2,128)S(1)} %get-tuple-element.426, f32[2,3840]{1,0:T(2,128)S(1)} %get-tuple-element.427), channel_id=1, replica_groups=mesh['dp'=8,'tok'=4] {'dp'}, use_global_device_ids=true, to_apply=%region_47.48 | all-reduce | flops 9216 | bytes 73728 | tf_op jit(solution)/shard_map/psum | solution.py:307
  910.7 366.9 %all-reduce.7.cloned.1.call-done = (f32[2,384,1152]{2,1,0:T(8,128)}, f32[2,384,384]{2,1,0:T(8,128)}, f32[2,384,1536]{2,1,0:T(8,128)}, f32[2,1536,384]{2,1,0:T(8,128)}) async-done(((f32[2,384,1152]{2,1,0:T(8,128)}, f32[2,384,384]{2,1,0:T(8,128)}, f32[2,384,1536]{2,1,0:T(8,128)}, f32[2,1536,384]{2,1,0:T(8,128)}), (f32[2,384,1152]{2,1,0:T(8,128)}, f32[2,384,384]{2,1,0:T(8,128)}, f32[2,384,1536]{2,1,0:T(8,128)}, ...) | async-done | bytes 14155792 | tf_op jit(solution)/shard_map/psum | solution.py:307
  1322.4 12.1 concatenate.67
  (586 shorter events, 266.6 us)
Async XLA Ops:
  7.2 65.6 %copy-start.1 = (bf16[4,200,384]{2,1,0:T(8,128)(2,1)S(1)}, bf16[4,200,384]{2,1,0:T(8,128)(2,1)}, u32[]{:S(2)}) copy-start(bf16[4,200,384]{2,1,0:T(8,128)(2,1)} %param.23) | copy-start | bytes 1843204
  7.2 71.7 %all-gather.5.cloned.1.call-start = ((), (), s32[]{:S(2)}) async-start(), calls=%async_computation.8 | async-start | bytes 1990656 | tf_op jit(solution)/shard_map/all_gather | solution.py:168
  69.6 9.2 copy-start.66
  72.8 6.1 copy-start.64
  97.2 5.5 copy-start.109
  97.2 34.3 %all-to-all-start = ((bf16[4,200,3,4,128]{4,1,2,0,3:T(8,128)(2,1)}), bf16[4,200,3,4,128]{4,1,2,0,3:T(8,128)(2,1)}, u32[]{:S(2)}, u32[]{:S(2)}) async-start(bf16[4,200,3,4,128]{4,1,2,0,3:T(8,128)(2,1)} %copy.334), calls=%async_computation | async-start | bytes 4915200 | tf_op jit(solution)/shard_map/all_to_all | solution.py:54
  101.9 98.7 %all-gather.7.cloned.1.call-start = ((), (), s32[]{:S(2)}) async-start(), calls=%async_computation.9 | async-start | bytes 2654208 | tf_op jit(solution)/shard_map/all_gather | solution.py:170
  149.6 9.0 copy-start
  152.5 41.4 %all-to-all-start.1 = ((bf16[16,200,1,128]{3,1,2,0:T(8,128)(2,1)}), bf16[16,200,1,128]{3,1,2,0:T(8,128)(2,1)}, u32[]{:S(2)}, u32[]{:S(2)}) async-start(bf16[16,200,1,128]{3,1,2,0:T(8,128)(2,1)} %copy.337), calls=%async_computation.1 | async-start | bytes 1638400 | tf_op jit(solution)/shard_map/all_to_all | solution.py:61
  156.7 58.5 %all-gather.9.cloned.1.call-start = ((), (), s32[]{:S(2)}) async-start(), calls=%async_computation.10 | async-start | bytes 2654208 | tf_op jit(solution)/shard_map/all_gather | solution.py:171
  160.9 39.7 %copy-start.85 = (f32[1536]{0:T(1024)}, f32[1536]{0:T(1024)S(1)}, u32[]{:S(2)}) copy-start(f32[1536]{0:T(1024)S(1)} %get-tuple-element.500) | copy-start | bytes 18436
  193.9 5.5 copy-start.24
  200.2 15.1 %copy-start.4 = (f32[800,384]{1,0:T(8,128)}, f32[800,384]{1,0:T(8,128)S(1)}, u32[]{:S(2)}) copy-start(f32[800,384]{1,0:T(8,128)S(1)} %get-tuple-element.482) | copy-start | bytes 3686404
  200.2 15.0 %copy-start.60 = (f32[800]{0:T(1024)}, f32[800]{0:T(1024)S(1)}, u32[]{:S(2)}) copy-start(f32[800]{0:T(1024)S(1)} %broadcast_multiply_fusion.10) | copy-start | bytes 9604
  200.5 14.7 %copy-start.62 = (f32[800]{0:T(1024)}, f32[800]{0:T(1024)S(1)}, u32[]{:S(2)}) copy-start(f32[800]{0:T(1024)S(1)} %add_rsqrt_fusion.2) | copy-start | bytes 9604
  200.6 14.6 %copy-start.108 = (f32[384]{0:T(512)S(1)}, f32[384]{0:T(512)}, u32[]{:S(2)}) copy-start(f32[384]{0:T(512)} %get-tuple-element.370) | copy-start | bytes 4612
  247.8 34.2 %all-to-all-start.2 = ((bf16[4,200,3,4,128]{4,1,2,0,3:T(8,128)(2,1)}), bf16[4,200,3,4,128]{4,1,2,0,3:T(8,128)(2,1)}, u32[]{:S(2)}, u32[]{:S(2)}) async-start(bf16[4,200,3,4,128]{4,1,2,0,3:T(8,128)(2,1)} %copy.342), calls=%async_computation.2 | async-start | bytes 4915200 | tf_op jit(solution)/shard_map/all_to_all | solution.py:54
  252.4 33.8 %copy-start.98 = (s32[4,4]{1,0:T(4,128)S(1)}, s32[4,4]{1,0:T(4,128)}, u32[]{:S(2)}) copy-start(s32[4,4]{1,0:T(4,128)} %get-tuple-element.796) | copy-start | bytes 196
  294.5 6.5 copy-start.110
  296.7 16.3 %all-to-all-start.3 = ((bf16[16,200,1,128]{3,1,2,0:T(8,128)(2,1)}), bf16[16,200,1,128]{3,1,2,0:T(8,128)(2,1)}, u32[]{:S(2)}, u32[]{:S(2)}) async-start(bf16[16,200,1,128]{3,1,2,0:T(8,128)(2,1)} %copy.345), calls=%async_computation.3 | async-start | bytes 1638400 | tf_op jit(solution)/shard_map/all_to_all | solution.py:61
  301.2 15.2 %copy-start.95 = (pred[800]{0:T(1024)(128)(4,1)}, pred[800]{0:T(1024)(128)(4,1)S(1)}, u32[]{:S(2)}) copy-start(pred[800]{0:T(1024)(128)(4,1)S(1)} %lt.134) | copy-start | bytes 2404
  324.1 19.7 %copy-start.6 = (f32[800,384]{1,0:T(8,128)}, f32[800,384]{1,0:T(8,128)S(1)}, u32[]{:S(2)}) copy-start(f32[800,384]{1,0:T(8,128)S(1)} %get-tuple-element.488) | copy-start | bytes 3686404
  324.5 12.8 copy-start.54
  324.6 12.8 copy-start.111
  359.1 16.3 %all-to-all-start.4 = ((bf16[4,200,4,128]{3,1,0,2:T(8,128)(2,1)}), bf16[4,200,4,128]{3,1,0,2:T(8,128)(2,1)}, u32[]{:S(2)}, u32[]{:S(2)}) async-start(bf16[4,200,4,128]{3,1,0,2:T(8,128)(2,1)} %copy.350), calls=%async_computation.4 | async-start | bytes 1638400 | tf_op jit(solution)/shard_map/all_to_all | solution.py:68
  407.8 34.3 %all-to-all-start.5 = ((bf16[16,200,3,1,128]{4,1,3,2,0:T(8,128)(2,1)}), bf16[16,200,3,1,128]{4,1,3,2,0:T(8,128)(2,1)}, u32[]{:S(2)}, u32[]{:S(2)}) async-start(bf16[16,200,3,1,128]{4,1,3,2,0:T(8,128)(2,1)} %copy.354), calls=%async_computation.5 | async-start | bytes 4915200 | tf_op jit(solution)/shard_map/all_to_all | solution.py:75
  453.3 5.5 copy-start.15
  464.1 8.6 copy-start.27
  464.6 5.9 copy-start.5
  464.6 5.9 copy-start.61
  464.6 5.9 copy-start.63
  464.6 5.9 copy-start.69
  464.6 5.9 copy-start.114
  483.0 16.3 %all-to-all-start.6 = ((bf16[4,200,4,128]{3,1,0,2:T(8,128)(2,1)}), bf16[4,200,4,128]{3,1,0,2:T(8,128)(2,1)}, u32[]{:S(2)}, u32[]{:S(2)}) async-start(bf16[4,200,4,128]{3,1,0,2:T(8,128)(2,1)} %copy.359), calls=%async_computation.6 | async-start | bytes 1638400 | tf_op jit(solution)/shard_map/all_to_all | solution.py:68
  530.3 34.3 %all-to-all-start.7 = ((bf16[16,200,3,1,128]{4,1,3,2,0:T(8,128)(2,1)}), bf16[16,200,3,1,128]{4,1,3,2,0:T(8,128)(2,1)}, u32[]{:S(2)}, u32[]{:S(2)}) async-start(bf16[16,200,3,1,128]{4,1,3,2,0:T(8,128)(2,1)} %copy.363), calls=%async_computation.7 | async-start | bytes 4915200 | tf_op jit(solution)/shard_map/all_to_all | solution.py:75
  535.0 296.6 %all-reduce.9.cloned.1.call-start = ((), (), s32[]{:S(2)}) async-start(), calls=%async_computation.12 | async-start | bytes 28311552 | tf_op jit(solution)/shard_map/psum | solution.py:308
  575.6 5.5 copy-start.53
  586.1 691.4 %all-reduce.7.cloned.1.call-start = ((), (), s32[]{:S(2)}) async-start(), calls=%async_computation.11 | async-start | bytes 28311552 | tf_op jit(solution)/shard_map/psum | solution.py:307
  840.5 5.4 copy-start.3
  853.7 54.1 %copy-start.10 = (f32[800,384]{1,0:T(8,128)S(1)}, f32[800,384]{1,0:T(8,128)}, u32[]{:S(2)}) copy-start(f32[800,384]{1,0:T(8,128)} %copy-done.8) | copy-start | bytes 3686404
  1277.5 5.8 copy-start.17
  1285.7 5.7 copy-start.78
  1285.7 5.7 copy-start.93
  1285.7 5.9 copy-start.88
  1285.7 5.9 copy-start.97
  1292.9 5.4 copy-start.31
  1292.9 5.4 copy-start.32
  1292.9 5.4 copy-start.33
  (84 other events, 256.7 us)
Sparse Core Ops, SparseCore 0:
  10.9 50.0 all-gather.4
  105.5 51.8 all-gather.6
  160.3 54.3 all-gather.8
  586.2 245.2 all-reduce.8
  836.1 441.4 all-reduce.6
